TPU v7x, 32 devices: a whole 2x2x4 slice. The times are simulated.
32 devices in a mesh: wide: 8 (over z, x), narrow: 4 (over y, core).
Axes of the slice: x: 2, y: 2, z: 4, core: 2. Of those that a mesh axis runs over, the one named last changes fastest.
Arguments:
- tokens: bfloat16 [32768, 768], P(('wide', 'narrow')), may hold values from -6 to 6
- norm1_gain: bfloat16 [768], P(('wide', 'narrow')), may hold values from 0.25 to 1.75
- norm1_bias: bfloat16 [768], P(('wide', 'narrow')), may hold values from -2.5 to 2.5
- qkv_weight: bfloat16 [768, 2304], P(('wide', 'narrow')), may hold values from -0.21875 to 0.21875
- qkv_bias: bfloat16 [1536], P(('wide', 'narrow')), may hold values from -2.5 to 2.5
- out_weight: bfloat16 [768, 768], P(('wide', 'narrow')), may hold values from -9 to 9
- out_bias: bfloat16 [768], P(('wide', 'narrow')), may hold values from -12 to 12
- norm2_gain: bfloat16 [768], P(('wide', 'narrow')), may hold values from 0.25 to 1.75
- norm2_bias: bfloat16 [768], P(('wide', 'narrow')), may hold values from -2.5 to 2.5
- fc_weight: bfloat16 [768, 3072], P(('wide', 'narrow')), may hold values from -0.21875 to 0.21875
- fc_bias: bfloat16 [3072], P(('wide', 'narrow')), may hold values from -3 to 3
- proj_weight: bfloat16 [3072, 768], P(('wide', 'narrow')), may hold values from -2.5 to 2.5
- proj_bias: bfloat16 [768], P(('wide', 'narrow')), may hold values from -12 to 12
- seq_lengths: int32 [32], P(('wide', 'narrow')), may hold values from 64 to 1024, as said below
- out_cotangent: bfloat16 [32768, 768], P(('wide', 'narrow')), may hold values from -6 to 6
Outputs:
- layer_out: bfloat16 [32768, 768], P(('wide', 'narrow'))
- input_grad: bfloat16 [32768, 768], P(('wide', 'narrow'))
- norm1_gain_grad: float32 [768], P(('wide', 'narrow'))
- norm1_bias_grad: float32 [768], P(('wide', 'narrow'))
- qkv_weight_grad: float32 [768, 2304], P(('wide', 'narrow'))
- qkv_bias_grad: float32 [1536], P(('wide', 'narrow'))
- out_weight_grad: float32 [768, 768], P(('wide', 'narrow'))
- out_bias_grad: float32 [768], P(('wide', 'narrow'))
- norm2_gain_grad: float32 [768], P(('wide', 'narrow'))
- norm2_bias_grad: float32 [768], P(('wide', 'narrow'))
- fc_weight_grad: float32 [768, 3072], P(('wide', 'narrow'))
- fc_bias_grad: float32 [3072], P(('wide', 'narrow'))
- proj_weight_grad: float32 [3072, 768], P(('wide', 'narrow'))
- proj_bias_grad: float32 [768], P(('wide', 'narrow'))
Inputs may be any that keep to these rules, and one draw needn't show every extreme that they name: Each slot holds one sequence of seq_lengths tokens from its first position on; the rest of the slot is padding. Some slot is full in every draw.
All inputs are finite; a program needn't handle non-finite values.
Results may differ from a plain program's by a relative error of at most 0.013.
Values may be sent and summed in bfloat16 or wider, within the bound.
No kernel may reach another device: no remote copies, remote signals or barrier semaphores. Data moves between devices by JAX's collectives and lax.ppermute only.
A program may use at most 256 MiB of HBM per device.

v0:
```python
import math
import jax
import jax.numpy as jnp
from jax import lax
from jax.sharding import PartitionSpec as P

D = 768
H = 12
HD = 64
branch_scale = 1.0 / math.sqrt(48.0)
norm_epsilon = 1e-05
masked_value = -1e30


def layer_norm(values_in, gain_vec, shift_vec):
    row_mean = jnp.mean(values_in, axis=-1, keepdims=True)
    centred = values_in - row_mean
    row_var = jnp.mean(centred * centred, axis=-1, keepdims=True)
    return centred * lax.rsqrt(row_var + norm_epsilon) * gain_vec + shift_vec


def gelu_tanh(pre_act):
    inner = 0.7978845608028654 * (pre_act + 0.044715 * pre_act * pre_act * pre_act)
    return 0.5 * pre_act * (1.0 + jnp.tanh(inner))


def product(left, right):
    return jnp.dot(left, right, preferred_element_type=jnp.float32)


def left_product(left, right):
    return lax.dot_general(
        left, right, (((0,), (0,)), ((), ())), preferred_element_type=jnp.float32
    )


def right_product(left, right):
    return lax.dot_general(
        left, right, (((1,), (1,)), ((), ())), preferred_element_type=jnp.float32
    )


def split_heads(packed_slot):
    slot_size = packed_slot.shape[0]
    query_rows = packed_slot[:, :D].reshape(slot_size, H, HD)
    key_rows = packed_slot[:, D : 2 * D].reshape(slot_size, H, HD)
    value_rows = packed_slot[:, 2 * D :].reshape(slot_size, H, HD)
    return (query_rows, key_rows, value_rows)


def block_scores(query_block, key_block, block_start):
    score_scale = 1.0 / math.sqrt(HD)
    raw_scores = (
        jnp.einsum("qhd,khd->hqk", query_block, key_block, preferred_element_type=jnp.float32)
        * score_scale
    )
    row_place = block_start + jnp.arange(query_block.shape[0])
    col_place = jnp.arange(key_block.shape[0])
    causal = col_place[None, :] <= row_place[:, None]
    return (jnp.where(causal[None], raw_scores, masked_value), causal)


def forward_block(query_block, key_block, value_block, block_start):
    scores, causal = block_scores(query_block, key_block, block_start)
    row_max = jnp.max(scores, axis=-1, keepdims=True)
    shifted = jnp.exp(scores - row_max)
    row_total = jnp.sum(shifted, axis=-1, keepdims=True)
    soft_probs = (shifted / row_total).astype(jnp.bfloat16)
    mixed_rows = jnp.einsum(
        "hqk,khd->qhd", soft_probs, value_block, preferred_element_type=jnp.float32
    )
    return (mixed_rows, (row_max + jnp.log(row_total))[:, :, 0])


def slot_forward(item):
    packed_slot, seq_length = item
    query_rows, key_rows, value_rows = split_heads(packed_slot)
    slot_size = packed_slot.shape[0]
    block_rows = min(512, slot_size)
    mixed_parts = []
    stats_parts = []
    for block_index in range(slot_size // block_rows):
        block_start = block_index * block_rows
        block_end = block_start + block_rows
        query_block = query_rows[block_start:block_end]
        key_block = key_rows[:block_end]
        value_block = value_rows[:block_end]

        def compute_block():
            return forward_block(query_block, key_block, value_block, block_start)

        mixed_block, block_stats = compute_block()
        mixed_parts.append(mixed_block)
        stats_parts.append(block_stats)
    mixed_rows = jnp.concatenate(mixed_parts, 0)
    valid_rows = (jnp.arange(slot_size) < seq_length).astype(jnp.float32)
    mixed_rows = mixed_rows * valid_rows[:, None, None]
    return (mixed_rows.reshape(slot_size, D), jnp.concatenate(stats_parts, 1))


def slot_backward(item):
    packed_slot, grad_slot, slot_stats, seq_length = item
    query_rows, key_rows, value_rows = split_heads(packed_slot)
    slot_size = packed_slot.shape[0]
    grad_rows = grad_slot.reshape(slot_size, H, HD)
    score_scale = 1.0 / math.sqrt(HD)
    block_rows = min(512, slot_size)
    query_parts = []
    key_grad = jnp.zeros((slot_size, H, HD), jnp.float32)
    value_grad = jnp.zeros((slot_size, H, HD), jnp.float32)
    for block_index in range(slot_size // block_rows):
        block_start = block_index * block_rows
        block_end = block_start + block_rows
        query_block = query_rows[block_start:block_end]
        key_block = key_rows[:block_end]
        value_block = value_rows[:block_end]
        grad_block = grad_rows[block_start:block_end]
        stats_block = slot_stats[:, block_start:block_end]

        def compute_block():
            scores, causal = block_scores(query_block, key_block, block_start)
            soft_probs = jnp.where(causal[None], jnp.exp(scores - stats_block[:, :, None]), 0.0)
            low_probs = soft_probs.astype(jnp.bfloat16)
            value_part = jnp.einsum(
                "hqk,qhd->khd", low_probs, grad_block, preferred_element_type=jnp.float32
            )
            prob_grad = jnp.einsum(
                "qhd,khd->hqk", grad_block, value_block, preferred_element_type=jnp.float32
            )
            row_delta = jnp.sum(soft_probs * prob_grad, axis=-1, keepdims=True)
            score_grad = (soft_probs * (prob_grad - row_delta)).astype(jnp.bfloat16)
            query_part = (
                jnp.einsum(
                    "hqk,khd->qhd", score_grad, key_block, preferred_element_type=jnp.float32
                )
                * score_scale
            )
            key_part = (
                jnp.einsum(
                    "hqk,qhd->khd", score_grad, query_block, preferred_element_type=jnp.float32
                )
                * score_scale
            )
            return (query_part, key_part, value_part)

        query_part, key_part, value_part = compute_block()
        pad_rows = ((0, slot_size - block_end), (0, 0), (0, 0))
        key_grad = key_grad + jnp.pad(key_part, pad_rows)
        value_grad = value_grad + jnp.pad(value_part, pad_rows)
        query_parts.append(query_part)
    query_grad = jnp.concatenate(query_parts, 0)
    return jnp.concatenate(
        [
            query_grad.reshape(slot_size, D),
            key_grad.reshape(slot_size, D),
            value_grad.reshape(slot_size, D),
        ],
        axis=1,
    )


def local(
    tokens,
    norm1_gain,
    norm1_bias,
    qkv_weight,
    qkv_bias,
    out_weight,
    out_bias,
    norm2_gain,
    norm2_bias,
    fc_weight,
    fc_bias,
    proj_weight,
    proj_bias,
    seq_lengths,
    out_cotangent,
):
    attn_full = (
        lax.all_gather(norm1_gain, ("wide", "narrow"), axis=0, tiled=True),
        lax.all_gather(norm1_bias, ("wide", "narrow"), axis=0, tiled=True),
        lax.all_gather(qkv_weight, ("wide", "narrow"), axis=0, tiled=True),
        lax.all_gather(qkv_bias, ("wide", "narrow"), axis=0, tiled=True),
        lax.all_gather(out_weight, ("wide", "narrow"), axis=0, tiled=True),
        lax.all_gather(out_bias, ("wide", "narrow"), axis=0, tiled=True),
    )
    gain_one, shift_one, qkv_full, qkv_bias_full, out_full, out_bias_full = attn_full
    slot_count = seq_lengths.shape[0]
    slot_size = tokens.shape[0] // slot_count
    position = jnp.arange(slot_size)
    valid_rows = (position[None, :] < seq_lengths[:, None]).reshape(-1, 1).astype(jnp.float32)
    input_rows = tokens.astype(jnp.float32)
    gain_one_f = gain_one.astype(jnp.float32)
    shift_one_f = shift_one.astype(jnp.float32)
    norm_one = layer_norm(input_rows, gain_one_f, shift_one_f)
    low_one = norm_one.astype(jnp.bfloat16)
    bias_full = jnp.concatenate(
        [
            qkv_bias_full[:D].astype(jnp.float32),
            jnp.zeros((D,), jnp.float32),
            qkv_bias_full[D:].astype(jnp.float32),
        ]
    )
    packed = (product(low_one, qkv_full) + bias_full).astype(jnp.bfloat16)
    slot_packed = packed.reshape(slot_count, slot_size, 3 * D)
    mixed_all, stats_all = lax.map(slot_forward, (slot_packed, seq_lengths))
    low_mixed = mixed_all.reshape(-1, D).astype(jnp.bfloat16)
    branch = product(low_mixed, out_full) + out_bias_full.astype(jnp.float32)
    middle = input_rows + branch_scale * branch
    mlp_full = (
        lax.all_gather(norm2_gain, ("wide", "narrow"), axis=0, tiled=True),
        lax.all_gather(norm2_bias, ("wide", "narrow"), axis=0, tiled=True),
        lax.all_gather(fc_weight, ("wide", "narrow"), axis=0, tiled=True),
        lax.all_gather(fc_bias, ("wide", "narrow"), axis=0, tiled=True),
        lax.all_gather(proj_weight, ("wide", "narrow"), axis=0, tiled=True),
        lax.all_gather(proj_bias, ("wide", "narrow"), axis=0, tiled=True),
    )
    gain_two, shift_two, fc_full, fc_bias_full, proj_full, proj_bias_full = mlp_full
    gain_two_f = gain_two.astype(jnp.float32)
    shift_two_f = shift_two.astype(jnp.float32)
    norm_two = layer_norm(middle, gain_two_f, shift_two_f)
    low_two = norm_two.astype(jnp.bfloat16)
    hidden = product(low_two, fc_full) + fc_bias_full.astype(jnp.float32)
    low_active = gelu_tanh(hidden).astype(jnp.bfloat16)
    second = product(low_active, proj_full) + proj_bias_full.astype(jnp.float32)
    layer_out = (middle + branch_scale * second).astype(jnp.bfloat16)
    mlp_back = (
        lax.all_gather(norm2_gain, ("wide", "narrow"), axis=0, tiled=True),
        lax.all_gather(norm2_bias, ("wide", "narrow"), axis=0, tiled=True),
        lax.all_gather(fc_weight, ("wide", "narrow"), axis=0, tiled=True),
        lax.all_gather(fc_bias, ("wide", "narrow"), axis=0, tiled=True),
        lax.all_gather(proj_weight, ("wide", "narrow"), axis=0, tiled=True),
        lax.all_gather(proj_bias, ("wide", "narrow"), axis=0, tiled=True),
    )
    fc_back = mlp_back[2]
    proj_back = mlp_back[4]
    cotangent = out_cotangent.astype(jnp.float32) * valid_rows
    grad_second = (branch_scale * cotangent).astype(jnp.bfloat16)
    proj_weight_term = left_product(low_active, grad_second)
    proj_bias_term = jnp.sum(grad_second.astype(jnp.float32), axis=0)
    grad_active = right_product(grad_second, proj_back)
    unused_value, gelu_pull = jax.vjp(gelu_tanh, hidden)
    grad_hidden = gelu_pull(grad_active)[0].astype(jnp.bfloat16)
    fc_weight_term = left_product(low_two, grad_hidden)
    fc_bias_term = jnp.sum(grad_hidden.astype(jnp.float32), axis=0)
    grad_norm_two = right_product(grad_hidden, fc_back)
    unused_norm, norm_two_pull = jax.vjp(layer_norm, middle, gain_two_f, shift_two_f)
    middle_part, gain_two_term, shift_two_term = norm_two_pull(grad_norm_two)
    grad_middle = cotangent + middle_part
    mlp_grads = (
        lax.psum_scatter(gain_two_term, ("wide", "narrow"), scatter_dimension=0, tiled=True),
        lax.psum_scatter(shift_two_term, ("wide", "narrow"), scatter_dimension=0, tiled=True),
        lax.psum_scatter(fc_weight_term, ("wide", "narrow"), scatter_dimension=0, tiled=True),
        lax.psum_scatter(fc_bias_term, ("wide", "narrow"), scatter_dimension=0, tiled=True),
        lax.psum_scatter(proj_weight_term, ("wide", "narrow"), scatter_dimension=0, tiled=True),
        lax.psum_scatter(proj_bias_term, ("wide", "narrow"), scatter_dimension=0, tiled=True),
    )
    attn_back = (
        lax.all_gather(norm1_gain, ("wide", "narrow"), axis=0, tiled=True),
        lax.all_gather(norm1_bias, ("wide", "narrow"), axis=0, tiled=True),
        lax.all_gather(qkv_weight, ("wide", "narrow"), axis=0, tiled=True),
        lax.all_gather(qkv_bias, ("wide", "narrow"), axis=0, tiled=True),
        lax.all_gather(out_weight, ("wide", "narrow"), axis=0, tiled=True),
        lax.all_gather(out_bias, ("wide", "narrow"), axis=0, tiled=True),
    )
    qkv_back = attn_back[2]
    out_back = attn_back[4]
    grad_branch = (branch_scale * grad_middle).astype(jnp.bfloat16)
    out_weight_term = left_product(low_mixed, grad_branch)
    out_bias_term = jnp.sum(grad_branch.astype(jnp.float32), axis=0)
    grad_mixed = right_product(grad_branch, out_back).astype(jnp.bfloat16) * valid_rows.astype(
        jnp.bfloat16
    )
    grad_packed = lax.map(
        slot_backward,
        (slot_packed, grad_mixed.reshape(slot_count, slot_size, D), stats_all, seq_lengths),
    )
    low_grad_packed = grad_packed.reshape(-1, 3 * D).astype(jnp.bfloat16)
    qkv_weight_term = left_product(low_one, low_grad_packed)
    column_sums = jnp.sum(low_grad_packed.astype(jnp.float32), axis=0)
    qkv_bias_term = jnp.concatenate([column_sums[:D], column_sums[2 * D :]])
    grad_norm_one = right_product(low_grad_packed, qkv_back)
    unused_first, norm_one_pull = jax.vjp(layer_norm, input_rows, gain_one_f, shift_one_f)
    input_part, gain_one_term, shift_one_term = norm_one_pull(grad_norm_one)
    input_grad = (grad_middle + input_part).astype(jnp.bfloat16)
    attn_grads = (
        lax.psum_scatter(gain_one_term, ("wide", "narrow"), scatter_dimension=0, tiled=True),
        lax.psum_scatter(shift_one_term, ("wide", "narrow"), scatter_dimension=0, tiled=True),
        lax.psum_scatter(qkv_weight_term, ("wide", "narrow"), scatter_dimension=0, tiled=True),
        lax.psum_scatter(qkv_bias_term, ("wide", "narrow"), scatter_dimension=0, tiled=True),
        lax.psum_scatter(out_weight_term, ("wide", "narrow"), scatter_dimension=0, tiled=True),
        lax.psum_scatter(out_bias_term, ("wide", "narrow"), scatter_dimension=0, tiled=True),
    )
    return (
        layer_out,
        input_grad,
        attn_grads[0],
        attn_grads[1],
        attn_grads[2],
        attn_grads[3],
        attn_grads[4],
        attn_grads[5],
        mlp_grads[0],
        mlp_grads[1],
        mlp_grads[2],
        mlp_grads[3],
        mlp_grads[4],
        mlp_grads[5],
    )


def solution(mesh):
    placed = (
        P(("wide", "narrow"), None),
        P(("wide", "narrow")),
        P(("wide", "narrow")),
        P(("wide", "narrow"), None),
        P(("wide", "narrow")),
        P(("wide", "narrow"), None),
        P(("wide", "narrow")),
        P(("wide", "narrow")),
        P(("wide", "narrow")),
        P(("wide", "narrow"), None),
        P(("wide", "narrow")),
        P(("wide", "narrow"), None),
        P(("wide", "narrow")),
        P(("wide", "narrow")),
        P(("wide", "narrow"), None),
    )
    return jax.shard_map(
        local,
        mesh=mesh,
        in_specs=placed,
        out_specs=(
            P(("wide", "narrow"), None),
            P(("wide", "narrow"), None),
            P(("wide", "narrow")),
            P(("wide", "narrow")),
            P(("wide", "narrow"), None),
            P(("wide", "narrow")),
            P(("wide", "narrow"), None),
            P(("wide", "narrow")),
            P(("wide", "narrow")),
            P(("wide", "narrow")),
            P(("wide", "narrow"), None),
            P(("wide", "narrow")),
            P(("wide", "narrow"), None),
            P(("wide", "narrow")),
        ),
        check_vma=False,
    )
```

profile of v0, /device:TPU:0, one launch (start us, length us, event | category | flops | bytes accessed | tf_op | source)
XLA Modules:
  0.0 832.8 jit_solution(7919244227806289655)
XLA Ops:
  17.8 0.8 dynamic-update-slice.6
  18.7 42.8 %all-reduce.19 = (bf16[768]{0:T(1024)(128)(2,1)S(1)}, bf16[1536]{0:T(1024)(128)(2,1)S(1)}, bf16[768]{0:T(1024)(128)(2,1)S(1)}, bf16[768]{0:T(1024)(128)(2,1)S(1)...) all-reduce(bf16[768]{0:T(1024)(128)(2,1)S(1)} %dynamic-update-slice, ...), channel_id=1, replica_groups=mesh['wide'=8,'narrow'=4] {'wide','narrow'}, use_global_device_ids=true, to_apply=%add.5 | all-reduce | flops 9216 | bytes 36864
  62.7 1.2 iota_compare_fusion
  63.9 1.7 copy.73
  67.0 1.7 copy.82
  68.7 5.4 all-gather.5.cloned.1.call-done
  74.1 6.4 add_convert_fusion
  80.5 1.7 fusion.72
  82.3 1.9 fusion.73
  84.1 2.7 copy.80
  86.8 2.3 copy.76
  89.1 2.3 copy.79
  91.4 2.3 copy.75
  93.7 2.3 copy.74
  96.1 2.7 copy.78
  98.8 3.4 fusion.14
  102.2 2.6 fusion.13
  104.8 2.0 copy-done
  106.8 14.6 %fusion.2 = (f32[12,512]{1,0:T(8,128)S(1)}, f32[12,512,1024]{2,1,0:T(8,128)}) fusion(pred[512,1024]{1,0:T(8,128)(4,1)} %iota_compare_fusion, bf16[512,12,64]{0,2,1:T(8,128)(2,1)} %bitcast.76, bf16[1024,12,64]{0,2,1:T(8,128)(2,1)} %bitcast.72), kind=kOutput, calls=%fused_computation.11 | convolution fusion | flops 824174592 | bytes 28073984 | tf_op jit(solution)/shard_map/while/body/eval_jaxpr/qhd,khd->hqk/dot_general | solution.py:54
  121.4 13.4 %fusion = f32[12,512]{1,0:T(8,128)S(1)} fusion(f32[12,512,1024]{2,1,0:T(8,128)} %get-tuple-element.124, f32[12,512]{1,0:T(8,128)S(1)} %get-tuple-element.123, pred[512,1024]{1,0:T(8,128)(4,1)S(1)} %copy-done.11), kind=kLoop, calls=%fused_computation.6 | loop fusion | flops 25159680 | bytes 25739264 | tf_op jit(solution)/shard_map/while/body/eval_jaxpr/reduce_sum | solution.py:67
  134.9 8.1 fusion.17
  143.8 1.2 slice-done.5
  145.0 9.7 %fusion.12 = f32[12,64,512]{2,1,0:T(8,128)} fusion(bf16[1024,12,64]{0,2,1:T(8,128)(2,1)} %bitcast.86, f32[12,512,1024]{2,1,0:T(8,128)S(1)} %bitcast.69, f32[12,512]{1,0:T(8,128)S(1)} %fusion, f32[12,512]{1,0:T(8,128)S(1)} %get-tuple-element.123, pred[512,1024]{1,0:T(8,128)(4,1)S(1)} %copy-done.11), kind=kOutput, calls=%fused_computation.29 | convolution fusion | flops 836763648 | bytes 28884992 | tf_op jit(solution)/shard_map/while/body/eval_jaxpr/hqk,khd->qhd/dot_general | solution.py:69
  154.7 5.6 fusion.76
  160.3 2.3 multiply_reduce_fusion.4
  163.3 32.1 %all-gather.9.cloned.1.call-done = bf16[768,3072]{1,0:T(8,128)(2,1)} async-done(((bf16[24,3072]{1,0:T(8,128)(2,1)}), bf16[768,3072]{1,0:T(8,128)(2,1)}) %all-gather.9.cloned.1.call-update) | async-done | bytes 4718608 | tf_op jit(solution)/shard_map/all_gather | solution.py:213
  195.4 11.0 %fusion.68 = f32[1024,3072]{1,0:T(8,128)} fusion(bf16[768,3072]{1,0:T(8,128)(2,1)} %all-gather.9.cloned.1.call-done, f32[1024,768]{0,1:T(8,128)} %get-tuple-element.128, f32[768]{0:T(1024)S(1)} %convert_element_type.145, f32[768]{0:T(1024)S(1)} %convert_element_type.144, f32[1024]{0:T(1024)S(1)} %fusion.47, f32[1024]{0:T(1024)S(1)} %broadcast_multiply_fusion), kind=kOutput, calls=%fused_computation.123 | convolution fusion | flops 4835770368 | bytes 20461568 | tf_op jit(solution)/shard_map/dot_general | solution.py:28
  206.4 54.2 %all-gather.11.cloned.1.call-done = bf16[3072,768]{1,0:T(8,128)(2,1)} async-done(((bf16[96,768]{1,0:T(8,128)(2,1)}), bf16[3072,768]{1,0:T(8,128)(2,1)}) %all-gather.11.cloned.1.call-update) | async-done | bytes 4718608 | tf_op jit(solution)/shard_map/all_gather | solution.py:215
  260.6 18.6 %convert_reduce_fusion = (f32[3072]{0:T(1024)}, bf16[1024,3072]{1,0:T(8,128)(2,1)S(1)}) fusion(f32[1024,3072]{1,0:T(8,128)} %fusion.68, f32[3072]{0:T(1024)S(1)} %copy-done.44, bf16[3072,768]{1,0:T(8,128)(2,1)} %all-gather.11.cloned.1.call-done, bf16[1024,768]{0,1:T(8,128)(2,1)S(1)} %copy.82, f32[1024]{0:T(1024)S(1)} %copy-done.32), kind=kOutput, calls=%fused_computation.18 | convolution fusion | flops 4919915520 | bytes 25194496 | tf_op jit(solution)/shard_map/dot_general | solution.py:38
  279.2 7.3 fusion.78
  286.6 2.5 copy.83
  289.1 3.4 multiply_reduce_fusion.2
  292.5 2.8 fusion.71
  295.4 1.6 convert_reduce_fusion.4
  297.0 0.9 copy-done.53
  298.4 2.9 fusion.42
  301.3 1.4 fusion.34
  302.8 7.8 fusion.35
  310.7 7.0 multiply_reduce_fusion.1
  317.8 10.2 %multiply_convert_fusion.1 = bf16[12,512,512]{1,2,0:T(8,128)(2,1)S(1)} fusion(f32[12,512,512]{1,2,0:T(8,128)} %get-tuple-element.130, f32[12,512]{1,0:T(8,128)S(1)} %get-tuple-element.129, f32[12,512]{1,0:T(8,128)S(1)} %copy-done.26, f32[12,512,512]{1,2,0:T(8,128)} %copy-done, pred[512,512]{0,1:T(8,128)(4,1)S(1)} %iota_compare_fusion.1), kind=kLoop, calls=%fused_computation.21 | loop fusion | flops 22020096 | bytes 31768576 | tf_op jit(solution)/shard_map/while/body/eval_jaxpr/convert_element_type | solution.py:131
  328.1 3.2 multiply_bitcast_fusion
  331.5 22.1 %multiply_reduce_fusion = (f32[12,512]{1,0:T(8,128)S(1)}, f32[12,512,1024]{2,1,0:T(8,128)}) fusion(f32[12,512]{1,0:T(8,128)S(1)} %log_add_fusion, f32[12,512,1024]{2,1,0:T(8,128)} %get-tuple-element.124, pred[512,1024]{1,0:T(8,128)(4,1)S(1)} %copy-done.12, bf16[512,12,64]{0,2,1:T(8,128)(2,1)S(1)} %bitcast.93, bf16[1024,12,64]{0,2,1:T(8,128)(2,1)S(1)} %bitcast.87), kind=kOutput, calls=%fused_computation.1 | convolution fusion | flops 843048960 | bytes 53264384 | tf_op jit(solution)/shard_map/while/body/eval_jaxpr/qhd,khd->hqk/dot_general | solution.py:127
  353.6 18.1 %multiply_convert_fusion = bf16[12,512,1024]{2,1,0:T(8,128)(2,1)S(1)} fusion(f32[12,512,1024]{2,1,0:T(8,128)} %get-tuple-element.132, f32[12,512]{1,0:T(8,128)S(1)} %get-tuple-element.131, f32[12,512]{1,0:T(8,128)S(1)} %log_add_fusion, f32[12,512,1024]{2,1,0:T(8,128)} %get-tuple-element.124, pred[512,1024]{1,0:T(8,128)(4,1)} %iota_compare_fusion), kind=kLoop, calls=%fused_computation | loop fusion | flops 44040192 | bytes 63488000 | tf_op jit(solution)/shard_map/while/body/eval_jaxpr/convert_element_type | solution.py:131
  371.7 6.2 fusion.38
  378.0 4.0 fusion.31
  382.0 4.6 fusion.39
  388.5 12.8 %fusion.30 = bf16[1024,12,64]{0,2,1:T(8,128)(2,1)S(1)} fusion(f32[512,12,64]{0,2,1:T(8,128)S(1)} %copy-done.56, bf16[512,12,64]{0,2,1:T(8,128)(2,1)S(1)} %bitcast.94, f32[12,512]{1,0:T(8,128)S(1)} %log_add_fusion, f32[12,512,1024]{2,1,0:T(8,128)} %get-tuple-element.124, pred[512,1024]{1,0:T(8,128)(4,1)S(1)} %copy-done.13), kind=kOutput, calls=%fused_computation.57 | convolution fusion | flops 838336512 | bytes 29646848 | tf_op jit(solution)/shard_map/while/body/eval_jaxpr/hqk,qhd->khd/dot_general | solution.py:124
  401.3 1.1 copy-done.19
  402.5 7.0 fusion.63
  409.6 1.3 copy-done.8
  410.9 14.1 %fusion.40 = f32[3072,768]{1,0:T(8,128)} fusion(bf16[1024,768]{0,1:T(8,128)(2,1)S(1)} %copy-done.8, f32[1024]{0:T(1024)S(1)} %copy-done.32, f32[1024,3072]{1,0:T(8,128)} %fusion.68, f32[3072]{0:T(1024)S(1)} %copy-done.44), kind=kOutput, calls=%fused_computation.83 | convolution fusion | flops 4866441216 | bytes 23609344 | tf_op jit(solution)/shard_map/dot_general | solution.py:32
  425.7 10.7 %fusion.67 = f32[768,3072]{1,0:T(8,128)} fusion(bf16[1024,3072]{1,0:T(8,128)(2,1)} %copy-done.55, f32[1024,768]{0,1:T(8,128)} %get-tuple-element.128, f32[768]{0:T(1024)S(1)} %copy-done.25, f32[768]{0:T(1024)S(1)} %convert_element_type.144, f32[1024]{0:T(1024)S(1)} %fusion.47, f32[1024]{0:T(1024)S(1)} %broadcast_multiply_fusion), kind=kOutput, calls=%fused_computation.122 | convolution fusion | flops 4835770368 | bytes 18888704 | tf_op jit(solution)/shard_map/dot_general | solution.py:32
  437.1 12.4 %add_convert_fusion.2 = bf16[1024,768]{0,1:T(8,128)(2,1)} fusion(f32[1024,768]{0,1:T(8,128)} %get-tuple-element.128, bf16[3072,768]{1,0:T(8,128)(2,1)} %all-gather.11.cloned.1.call-done, f32[768]{0:T(1024)S(1)} %convert_element_type.149, f32[1024,3072]{1,0:T(8,128)} %fusion.68, f32[3072]{0:T(1024)S(1)} %copy-done.44), kind=kOutput, calls=%fused_computation.69 | convolution fusion | flops 4866441216 | bytes 22035456 | tf_op jit(solution)/shard_map/dot_general | solution.py:28
  449.4 2.6 copy.90
  452.0 9.2 %fusion.77 = (f32[768]{0:T(1024)S(1)}, f32[1024,768]{1,0:T(8,128)}) fusion(bf16[768,2304]{1,0:T(8,128)(2,1)} %all-gather.5.cloned.1.call-done, bf16[1024,768]{0,1:T(8,128)(2,1)} %bitcast.89, bf16[1024,768]{0,1:T(8,128)(2,1)} %bitcast.79, bf16[1024,768]{0,1:T(8,128)(2,1)} %bitcast.84), kind=kOutput, calls=%fused_computation.130 | convolution fusion | flops 3638820096 | bytes 11406336 | tf_op jit(solution)/shard_map/dot_general | solution.py:38
  461.3 3.6 copy.87
  464.9 3.1 convert_reduce_fusion.1
  468.9 1.3 fusion.26
  470.2 41.3 %all-reduce.18 = (f32[768]{0:T(1024)S(1)}, f32[768]{0:T(1024)S(1)}, f32[1536]{0:T(1024)S(1)}, f32[768]{0:T(1024)S(1)}, f32[768]{0:T(1024)S(1)}, /*index=5*/f32[7...) all-reduce(f32[768]{0:T(1024)S(1)} %get-tuple-element.88, ...), channel_id=2, replica_groups=mesh['wide'=8,'narrow'=4] {'wide','narrow'}, use_global_device_ids=true, to_apply=%region_15.16.clone | all-reduce | flops 9216 | bytes 73728
  515.1 5.7 add_convert_fusion.1
  520.8 2.6 copy.91
  524.5 17.9 %reduce-scatter.5.cloned.1.call-done = f32[24,2304]{1,0:T(8,128)} async-done(((f32[768,2304]{1,0:T(8,128)}), f32[24,2304]{1,0:T(8,128)}) %reduce-scatter.5.cloned.1.call-update) | async-done | bytes 221200 | tf_op jit(solution)/shard_map/reduce_scatter | solution.py:289
  542.5 141.2 %reduce-scatter.11.cloned.1.call-done = f32[96,768]{1,0:T(8,128)} async-done(((f32[3072,768]{1,0:T(8,128)}), f32[96,768]{1,0:T(8,128)}) %reduce-scatter.11.cloned.1.call-update) | async-done | bytes 294928 | tf_op jit(solution)/shard_map/reduce_scatter | solution.py:255
  683.7 142.0 %reduce-scatter.9.cloned.1.call-done = f32[24,3072]{1,0:T(8,128)} async-done(((f32[768,3072]{1,0:T(8,128)}), f32[24,3072]{1,0:T(8,128)}) %reduce-scatter.9.cloned.1.call-update) | async-done | bytes 294928 | tf_op jit(solution)/shard_map/reduce_scatter | solution.py:253
  (201 shorter events, 23.7 us)
Async XLA Ops:
  7.2 66.9 %all-gather.5.cloned.1.call-start = ((), (), s32[]{:S(2)}) async-start(), calls=%async_computation.4 | async-start | bytes 3649536 | tf_op jit(solution)/shard_map/all_gather | solution.py:182
  7.9 146.8 %all-gather.7.cloned.1.call-start = ((), (), s32[]{:S(2)}) async-start(), calls=%async_computation.5 | async-start | bytes 1216512 | tf_op jit(solution)/shard_map/all_gather | solution.py:184
  8.7 186.7 %all-gather.9.cloned.1.call-start = ((), (), s32[]{:S(2)}) async-start(), calls=%async_computation.6 | async-start | bytes 4866048 | tf_op jit(solution)/shard_map/all_gather | solution.py:213
  9.4 251.2 %all-gather.11.cloned.1.call-start = ((), (), s32[]{:S(2)}) async-start(), calls=%async_computation.7 | async-start | bytes 4866048 | tf_op jit(solution)/shard_map/all_gather | solution.py:215
  10.0 514.5 %reduce-scatter.7.cloned.1.call-start = ((), (), s32[]{:S(2)}) async-start(), calls=%async_computation.9 | async-start | bytes 2433024 | tf_op jit(solution)/shard_map/reduce_scatter | solution.py:291
  62.1 12.1 %copy-start.29 = (f32[768]{0:T(1024)}, f32[768]{0:T(1024)S(1)}, u32[]{:S(2)}) copy-start(f32[768]{0:T(1024)S(1)} %convert_element_type.133) | copy-start | bytes 9220
  62.1 12.1 %copy-start.46 = (f32[768]{0:T(1024)}, f32[768]{0:T(1024)S(1)}, u32[]{:S(2)}) copy-start(f32[768]{0:T(1024)S(1)} %convert_element_type.134) | copy-start | bytes 9220
  62.1 133.3 %copy-start.24 = (f32[768]{0:T(1024)}, f32[768]{0:T(1024)S(1)}, u32[]{:S(2)}) copy-start(f32[768]{0:T(1024)S(1)} %convert_element_type.145) | copy-start | bytes 9220
  65.6 89.1 %copy-start.2 = (bf16[1024,768]{0,1:T(8,128)(2,1)}, bf16[1024,768]{0,1:T(8,128)(2,1)S(1)}, u32[]{:S(2)}) copy-start(bf16[1024,768]{0,1:T(8,128)(2,1)S(1)} %copy.73) | copy-start | bytes 4718596
  65.9 14.6 %copy-start.27 = (f32[1024]{0:T(1024)}, f32[1024]{0:T(1024)S(1)}, u32[]{:S(2)}) copy-start(f32[1024]{0:T(1024)S(1)} %broadcast_multiply_fusion.1) | copy-start | bytes 12292
  66.9 13.6 %copy-start.33 = (f32[1024]{0:T(1024)}, f32[1024]{0:T(1024)S(1)}, u32[]{:S(2)}) copy-start(f32[1024]{0:T(1024)S(1)} %fusion.46) | copy-start | bytes 12292
  68.7 191.9 %copy-start.6 = (bf16[1024,768]{0,1:T(8,128)(2,1)}, bf16[1024,768]{0,1:T(8,128)(2,1)S(1)}, u32[]{:S(2)}) copy-start(bf16[1024,768]{0,1:T(8,128)(2,1)S(1)} %copy.82) | copy-start | bytes 4718596
  102.2 4.6 copy-start
  106.8 14.6 %copy-start.11 = (pred[512,1024]{1,0:T(8,128)(4,1)S(1)}, pred[512,1024]{1,0:T(8,128)(4,1)}, u32[]{:S(2)}) copy-start(pred[512,1024]{1,0:T(8,128)(4,1)} %iota_compare_fusion) | copy-start | bytes 1572868
  121.4 13.4 %copy-start.20 = (bf16[512,768]{0,1:T(8,128)(2,1)S(1)}, bf16[512,768]{0,1:T(8,128)(2,1)}, u32[]{:S(2)}) copy-start(bf16[512,768]{0,1:T(8,128)(2,1)} %copy.74) | copy-start | bytes 2359300
  121.4 21.6 %slice-start = ((s8[25165824]{0:T(1024)(128)(4,1)}), s8[4194304]{0:T(1024)(128)(4,1)S(1)}, s32[]{:S(2)}) async-start(s8[25165824]{0:T(1024)(128)(4,1)} %bitcast.68), calls=%async_computation.12 | async-start | bytes 8388608
  121.4 21.6 %slice-start.1 = ((s8[25165824]{0:T(1024)(128)(4,1)}), s8[4194304]{0:T(1024)(128)(4,1)S(1)}, s32[]{:S(2)}) async-start(s8[25165824]{0:T(1024)(128)(4,1)} %bitcast.68), calls=%async_computation.13 | async-start | bytes 8388608
  134.8 8.2 slice-start.2
  134.9 8.2 slice-start.3
  134.9 9.0 %slice-start.4 = ((s8[25165824]{0:T(1024)(128)(4,1)}), s8[4194304]{0:T(1024)(128)(4,1)S(1)}, s32[]{:S(2)}) async-start(s8[25165824]{0:T(1024)(128)(4,1)} %bitcast.68), calls=%async_computation.16 | async-start | bytes 8388608
  134.9 10.2 %slice-start.5 = ((s8[25165824]{0:T(1024)(128)(4,1)}), s8[4194304]{0:T(1024)(128)(4,1)S(1)}, s32[]{:S(2)}) async-start(s8[25165824]{0:T(1024)(128)(4,1)} %bitcast.68), calls=%async_computation.17 | async-start | bytes 8388608
  145.0 9.7 %copy-start.31 = (f32[1024]{0:T(1024)S(1)}, f32[1024]{0:T(1024)}, u32[]{:S(2)}) copy-start(f32[1024]{0:T(1024)} %fusion.45) | copy-start | bytes 12292
  145.0 9.7 %copy-start.48 = (f32[768]{0:T(1024)S(1)}, f32[768]{0:T(1024)}, u32[]{:S(2)}) copy-start(f32[768]{0:T(1024)} %convert_element_type.143) | copy-start | bytes 9220
  163.2 97.4 %copy-start.32 = (f32[1024]{0:T(1024)S(1)}, f32[1024]{0:T(1024)}, u32[]{:S(2)}) copy-start(f32[1024]{0:T(1024)} %fusion.45) | copy-start | bytes 12292
  163.2 97.4 %copy-start.44 = (f32[3072]{0:T(1024)S(1)}, f32[3072]{0:T(1024)}, u32[]{:S(2)}) copy-start(f32[3072]{0:T(1024)} %convert_element_type.147) | copy-start | bytes 36868
  260.6 18.6 %copy-start.16 = (bf16[768,3072]{1,0:T(8,128)(2,1)S(1)}, bf16[768,3072]{1,0:T(8,128)(2,1)}, u32[]{:S(2)}) copy-start(bf16[768,3072]{1,0:T(8,128)(2,1)} %all-gather.9.cloned.1.call-done) | copy-start | bytes 14155780
  279.2 7.3 copy-start.55
  289.1 3.4 copy-start.40
  292.5 2.9 copy-start.7
  295.3 1.7 copy-start.5
  295.4 1.7 copy-start.35
  295.4 2.5 copy-start.53
  295.4 3.0 copy-start.54
  298.4 2.9 copy-start.51
  298.4 2.9 copy-start.52
  301.3 1.5 copy-start.26
  301.3 9.4 %slice-start.6 = ((s8[12582912]{0:T(1024)(128)(4,1)}), s8[4194304]{0:T(1024)(128)(4,1)S(1)}, s32[]{:S(2)}) async-start(s8[12582912]{0:T(1024)(128)(4,1)} %bitcast.70), calls=%async_computation.18 | async-start | bytes 8388608
  302.7 8.0 slice-start.7
  302.8 28.7 %copy-start.22 = (bf16[512,768]{0,1:T(8,128)(2,1)}, bf16[512,768]{0,1:T(8,128)(2,1)S(1)}, u32[]{:S(2)}) copy-start(bf16[512,768]{0,1:T(8,128)(2,1)S(1)} %get-tuple-element.117) | copy-start | bytes 2359300
  302.8 7.9 slice-start.8
  302.8 7.9 copy-start.21
  317.8 224.7 %reduce-scatter.5.cloned.1.call-start = ((), (), s32[]{:S(2)}) async-start(), calls=%async_computation.8 | async-start | bytes 7299072 | tf_op jit(solution)/shard_map/reduce_scatter | solution.py:289
  317.8 10.2 %copy-start.14 = (bf16[512,768]{0,1:T(8,128)(2,1)S(1)}, bf16[512,768]{0,1:T(8,128)(2,1)}, u32[]{:S(2)}) copy-start(bf16[512,768]{0,1:T(8,128)(2,1)} %copy.75) | copy-start | bytes 2359300
  328.0 3.4 copy-start.1
  328.1 3.4 copy-start.12
  328.1 3.4 copy-start.18
  378.0 4.0 copy-start.9
  382.0 19.3 %copy-start.10 = (bf16[1024,12,64]{0,2,1:T(8,128)(2,1)}, bf16[1024,12,64]{0,2,1:T(8,128)(2,1)S(1)}, u32[]{:S(2)}) copy-start(bf16[1024,12,64]{0,2,1:T(8,128)(2,1)S(1)} %fusion.31) | copy-start | bytes 4718596
  382.0 4.6 copy-start.17
  386.7 1.8 copy-start.56
  388.5 12.8 %copy-start.15 = (bf16[1024,12,64]{0,2,1:T(8,128)(2,1)}, bf16[1024,12,64]{0,2,1:T(8,128)(2,1)S(1)}, u32[]{:S(2)}) copy-start(bf16[1024,12,64]{0,2,1:T(8,128)(2,1)S(1)} %pad_maximum_fusion.1) | copy-start | bytes 4718596
  388.5 14.0 %copy-start.3 = (bf16[1024,768]{0,1:T(8,128)(2,1)S(1)}, bf16[1024,768]{0,1:T(8,128)(2,1)}, u32[]{:S(2)}) copy-start(bf16[1024,768]{0,1:T(8,128)(2,1)} %copy-done.2) | copy-start | bytes 4718596
  388.5 14.0 %copy-start.28 = (f32[1024]{0:T(1024)S(1)}, f32[1024]{0:T(1024)}, u32[]{:S(2)}) copy-start(f32[1024]{0:T(1024)} %copy-done.27) | copy-start | bytes 12292
  388.5 14.0 %copy-start.30 = (f32[768]{0:T(1024)S(1)}, f32[768]{0:T(1024)}, u32[]{:S(2)}) copy-start(f32[768]{0:T(1024)} %copy-done.29) | copy-start | bytes 9220
  388.5 14.0 %copy-start.34 = (f32[1024]{0:T(1024)S(1)}, f32[1024]{0:T(1024)}, u32[]{:S(2)}) copy-start(f32[1024]{0:T(1024)} %copy-done.33) | copy-start | bytes 12292
  388.5 14.0 %copy-start.47 = (f32[768]{0:T(1024)S(1)}, f32[768]{0:T(1024)}, u32[]{:S(2)}) copy-start(f32[768]{0:T(1024)} %copy-done.46) | copy-start | bytes 9220
  409.5 274.1 %reduce-scatter.11.cloned.1.call-start = ((), (), s32[]{:S(2)}) async-start(), calls=%async_computation.11 | async-start | bytes 9732096 | tf_op jit(solution)/shard_map/reduce_scatter | solution.py:255
  425.1 400.6 %reduce-scatter.9.cloned.1.call-start = ((), (), s32[]{:S(2)}) async-start(), calls=%async_computation.10 | async-start | bytes 9732096 | tf_op jit(solution)/shard_map/reduce_scatter | solution.py:253
  464.9 3.3 copy-start.4
  468.8 1.4 copy-start.41
  468.8 1.4 copy-start.42
  468.8 1.4 copy-start.43
  468.8 1.4 copy-start.45
  468.8 46.3 %copy-start.36 = (f32[1024]{0:T(1024)S(1)}, f32[1024]{0:T(1024)}, u32[]{:S(2)}) copy-start(f32[1024]{0:T(1024)} %copy-done.35) | copy-start | bytes 12292
  (10 other events, 9.7 us)
Sparse Core Ops, SparseCore 0:
  10.9 63.1 all-gather.4
  77.0 52.8 all-gather.6
  132.8 62.5 all-gather.8
  198.2 62.3 all-gather.10
  317.9 97.8 reduce-scatter.6
  422.8 119.5 reduce-scatter.4
  548.9 134.7 reduce-scatter.10
  691.2 134.4 reduce-scatter.8
where the time goes:
time: 840 us; the launch traced here: 833 us
  waiting for transfers between devices  396 us (47%)
  matrix products  210 us (25%)
  blocking collectives  84.1 us (10%)
  other arithmetic  70.2 us (8%)
  local copies, waits for them, and re-layouts  56.5 us (7%)
  between operations  15.9 us (2%)
    reduce_scatter x1, waiting for transfers between devices, local(): lax.psum_scatter(fc_weight_term, ('wide', 'narrow'), scatter_dimension=0,...  142 us
    reduce_scatter x1, waiting for transfers between devices, local(): lax.psum_scatter(proj_weight_term, ('wide', 'narrow'), scatter_dimension=...  141 us
    unnamed x2, blocking collectives  84.1 us
    all_gather x1, waiting for transfers between devices, local(): lax.all_gather(proj_weight, ('wide', 'narrow'), axis=0, tiled=True)  54.2 us
    dot_general x4, matrix products, right_product(): lax.dot_general(left, right, (((1,), (1,)), ((), ())), preferred_element_...  36.6 us
    dot_general x4, matrix products, product(): return jnp.dot(left, right, preferred_element_type=jnp.float32)  35.3 us
    dot_general x4, matrix products, left_product(): lax.dot_general(left, right, (((0,), (0,)), ((), ())), preferred_element_...  34.7 us
    all_gather x1, waiting for transfers between devices, local(): lax.all_gather(fc_weight, ('wide', 'narrow'), axis=0, tiled=True)  32.1 us
  transfers between devices with their start and end apart: 8, of which 6 were waited for; matrix products, arithmetic and copies ran while one was open for 32% of the time, Pallas kernels for 0%

commit v1 on v0

--- a/solution.py
+++ b/solution.py
@@ -10,6 +10,18 @@
 branch_scale = 1.0 / math.sqrt(48.0)
 norm_epsilon = 1e-05
 masked_value = -1e30
+
+
+def gather_by_bits(array, axis, dim):
+    ways, here = (lax.axis_size(axis), lax.axis_index(axis))
+    grown, reach = (array, 1)
+    while reach < ways:
+        theirs = lax.ppermute(grown, axis, [(d, d ^ reach) for d in range(ways)])
+        mine_first = jnp.concatenate([grown, theirs], axis=dim)
+        theirs_first = jnp.concatenate([theirs, grown], axis=dim)
+        grown = jnp.where(here & reach == 0, mine_first, theirs_first)
+        reach = 2 * reach
+    return grown
 
 
 def layer_norm(values_in, gain_vec, shift_vec):
@@ -210,7 +222,7 @@
     mlp_full = (
         lax.all_gather(norm2_gain, ("wide", "narrow"), axis=0, tiled=True),
         lax.all_gather(norm2_bias, ("wide", "narrow"), axis=0, tiled=True),
-        lax.all_gather(fc_weight, ("wide", "narrow"), axis=0, tiled=True),
+        gather_by_bits(fc_weight, ("wide", "narrow"), 0),
         lax.all_gather(fc_bias, ("wide", "narrow"), axis=0, tiled=True),
         lax.all_gather(proj_weight, ("wide", "narrow"), axis=0, tiled=True),
         lax.all_gather(proj_bias, ("wide", "narrow"), axis=0, tiled=True),

time: 840 us -> 914 us (1.088)
  waiting for transfers between devices: 396 us -> 456 us
    ppermute x0 -> x5, waiting for transfers between devices: none -> 34.6 us  [gather_by_bits(): theirs = lax.ppermute(grown, axis, [(d, d ^ reach) for d in range(ways)])]
    all_gather x1, waiting for transfers between devices: 0.01 us -> 26.8 us  [local(): lax.all_gather(out_weight, ('wide', 'narrow'), axis=0, tiled=True)]
    all_gather x1, waiting for transfers between devices: 32.1 us -> 44.9 us  [local(): lax.all_gather(fc_weight, ('wide', 'narrow'), axis=0, tiled=True)]
    all_gather x1, waiting for transfers between devices: 54.2 us -> 44.9 us  [local(): lax.all_gather(proj_weight, ('wide', 'narrow'), axis=0, tiled=True)]
    unnamed x160 -> x148, local copies, waits for them, and re-layouts: 32 us -> 30.7 us
  transfers between devices with their start and end apart: 8 -> 13, of which waited for: 6 -> 9; matrix products, arithmetic and copies ran while one was open for 32% -> 32% of each run, Pallas kernels for 0% -> 0%
where the time goes in v1:
time: 914 us; the launch traced here: 906 us
  waiting for transfers between devices  456 us (50%)
  matrix products  216 us (24%)
  blocking collectives  82.6 us (9%)
  other arithmetic  71.5 us (8%)
  local copies, waits for them, and re-layouts  56.4 us (6%)
  between operations  15.9 us (2%)
    reduce_scatter x1, waiting for transfers between devices, local(): lax.psum_scatter(fc_weight_term, ('wide', 'narrow'), scatter_dimension=0,...  142 us
    reduce_scatter x1, waiting for transfers between devices, local(): lax.psum_scatter(proj_weight_term, ('wide', 'narrow'), scatter_dimension=...  141 us
    unnamed x2, blocking collectives  82.6 us
    all_gather x1, waiting for transfers between devices, local(): lax.all_gather(fc_weight, ('wide', 'narrow'), axis=0, tiled=True)  44.9 us
    all_gather x1, waiting for transfers between devices, local(): lax.all_gather(proj_weight, ('wide', 'narrow'), axis=0, tiled=True)  44.9 us
    dot_general x4, matrix products, right_product(): lax.dot_general(left, right, (((1,), (1,)), ((), ())), preferred_element_...  41.3 us
    dot_general x4, matrix products, product(): return jnp.dot(left, right, preferred_element_type=jnp.float32)  36.5 us
    dot_general x4, matrix products, left_product(): lax.dot_general(left, right, (((0,), (0,)), ((), ())), preferred_element_...  34.6 us
  transfers between devices with their start and end apart: 13, of which 9 were waited for; matrix products, arithmetic and copies ran while one was open for 32% of the time, Pallas kernels for 0%

profile of v1, /device:TPU:0, one launch (start us, length us, event | category | flops | bytes accessed | tf_op | source)
XLA Modules:
  0.0 905.9 jit_solution(2582523267955321520)
XLA Ops:
  12.2 2.9 collective-permute-start.1
  15.3 7.2 collective-permute-done.1
  23.4 1.7 collective-permute-start.2
  32.5 41.1 %all-reduce.19 = (bf16[768]{0:T(1024)(128)(2,1)S(1)}, bf16[1536]{0:T(1024)(128)(2,1)S(1)}, bf16[768]{0:T(1024)(128)(2,1)S(1)}, bf16[768]{0:T(1024)(128)(2,1)S(1)...) all-reduce(bf16[768]{0:T(1024)(128)(2,1)S(1)} %dynamic-update-slice, ...), channel_id=1, replica_groups=mesh['wide'=8,'narrow'=4] {'wide','narrow'}, use_global_device_ids=true, to_apply=%add.5 | all-reduce | flops 9216 | bytes 36864
  75.6 2.3 copy.82
  78.1 2.4 maximum_select_fusion.3
  83.9 26.1 %collective-permute-done.3 = bf16[192,3072]{1,0:T(8,128)(2,1)S(1)} collective-permute-done((bf16[192,3072]{1,0:T(8,128)(2,1)S(1)}, bf16[192,3072]{1,0:T(8,128)(2,1)S(1)}, u32[]{:S(2)}, u32[]{:S(2)}) %collective-permute-start.3) | collective-permute-done | bytes 1179680 | tf_op jit(solution)/shard_map/ppermute | solution.py:19
  110.0 1.9 maximum_select_fusion.2
  111.9 1.5 collective-permute-start.4
  113.4 6.4 add_convert_fusion
  119.8 1.7 fusion.79
  121.5 1.9 fusion.80
  123.4 2.7 copy.80
  126.1 2.3 copy.76
  128.4 2.3 copy.79
  130.7 2.3 copy.75
  133.0 2.3 copy.74
  135.3 2.7 copy.78
  138.0 3.4 fusion.14
  141.5 2.6 fusion.13
  144.0 2.0 copy-done.1
  146.1 14.4 %fusion.2 = (f32[12,512]{1,0:T(8,128)S(1)}, f32[12,512,1024]{2,1,0:T(8,128)}) fusion(pred[512,1024]{1,0:T(8,128)(4,1)} %iota_compare_fusion, bf16[512,12,64]{0,2,1:T(8,128)(2,1)} %bitcast.73, bf16[1024,12,64]{0,2,1:T(8,128)(2,1)} %bitcast.69), kind=kOutput, calls=%fused_computation.11 | convolution fusion | flops 824174592 | bytes 28073984 | tf_op jit(solution)/shard_map/while/body/eval_jaxpr/qhd,khd->hqk/dot_general | solution.py:66
  160.5 12.4 %fusion = f32[12,512]{1,0:T(8,128)S(1)} fusion(f32[12,512,1024]{2,1,0:T(8,128)} %get-tuple-element.124, f32[12,512]{1,0:T(8,128)S(1)} %get-tuple-element.123, pred[512,1024]{1,0:T(8,128)(4,1)S(1)} %copy-done.15), kind=kLoop, calls=%fused_computation.6 | loop fusion | flops 25159680 | bytes 25739264 | tf_op jit(solution)/shard_map/while/body/eval_jaxpr/reduce_sum | solution.py:79
  172.9 3.1 copy-done
  176.0 9.9 %fusion.12 = f32[12,64,512]{2,1,0:T(8,128)} fusion(bf16[1024,12,64]{0,2,1:T(8,128)(2,1)} %bitcast.83, f32[12,512,1024]{2,1,0:T(8,128)S(1)} %copy-done, f32[12,512]{1,0:T(8,128)S(1)} %fusion, f32[12,512]{1,0:T(8,128)S(1)} %get-tuple-element.123, pred[512,1024]{1,0:T(8,128)(4,1)S(1)} %copy-done.15), kind=kOutput, calls=%fused_computation.29 | convolution fusion | flops 836763648 | bytes 28884992 | tf_op jit(solution)/shard_map/while/body/eval_jaxpr/hqk,khd->qhd/dot_general | solution.py:81
  185.8 7.7 fusion.17
  193.6 26.8 %all-gather.7.cloned.1.call-done = bf16[768,768]{1,0:T(8,128)(2,1)} async-done(((bf16[24,768]{1,0:T(8,128)(2,1)}), bf16[768,768]{1,0:T(8,128)(2,1)}) %all-gather.7.cloned.1.call-update) | async-done | bytes 1179664 | tf_op jit(solution)/shard_map/all_gather | solution.py:196
  220.4 4.0 fusion.83
  226.1 13.8 %fusion.22 = f32[1024,3072]{1,0:T(8,128)} fusion(bf16[384,3072]{1,0:T(8,128)(2,1)} %collective-permute-done.4, bf16[384,3072]{1,0:T(8,128)(2,1)} %maximum_select_fusion.2, pred[]{:T(512)S(6)} %eq.15, f32[1024,768]{0,1:T(8,128)S(1)} %get-tuple-element.128, f32[768]{0:T(1024)S(1)} %copy-done.46, f32[768]{0:T(1024)S(1)} %convert_element_type.144, ...), kind=kOutput, calls=%fused_computation.47 | convolution fusion | flops 4857004032 | bytes 20461568 | tf_op jit(solution)/shard_map/dot_general | solution.py:40
  239.9 44.9 %all-gather.9.cloned.1.call-done = bf16[3072,768]{1,0:T(8,128)(2,1)} async-done(((bf16[96,768]{1,0:T(8,128)(2,1)}), bf16[3072,768]{1,0:T(8,128)(2,1)}) %all-gather.9.cloned.1.call-update) | async-done | bytes 4718608 | tf_op jit(solution)/shard_map/all_gather | solution.py:227
  284.7 20.3 %convert_reduce_fusion = (f32[3072]{0:T(1024)}, bf16[1024,3072]{1,0:T(8,128)(2,1)}) fusion(f32[1024,3072]{1,0:T(8,128)} %fusion.22, f32[3072]{0:T(1024)S(1)} %copy-done.44, bf16[3072,768]{1,0:T(8,128)(2,1)} %all-gather.9.cloned.1.call-done, bf16[1024,768]{0,1:T(8,128)(2,1)S(1)} %copy.82, f32[1024]{0:T(1024)S(1)} %fusion.52), kind=kOutput, calls=%fused_computation.18 | convolution fusion | flops 4919915520 | bytes 25194496 | tf_op jit(solution)/shard_map/dot_general | solution.py:50
  305.0 44.9 %all-gather.11.cloned.1.call-done = bf16[768,3072]{1,0:T(8,128)(2,1)} async-done(((bf16[24,3072]{1,0:T(8,128)(2,1)}), bf16[768,3072]{1,0:T(8,128)(2,1)}) %all-gather.11.cloned.1.call-update) | async-done | bytes 4718608 | tf_op jit(solution)/shard_map/all_gather | solution.py:242
  349.9 10.4 %fusion.85 = (f32[768]{0:T(1024)}, f32[1024,768]{1,0:T(8,128)}) fusion(bf16[1024,3072]{1,0:T(8,128)(2,1)} %get-tuple-element.138, bf16[768,3072]{1,0:T(8,128)(2,1)} %all-gather.11.cloned.1.call-done), kind=kOutput, calls=%fused_computation.143 | convolution fusion | flops 4832623616 | bytes 14158848 | tf_op jit(solution)/shard_map/dot_general | solution.py:50
  360.3 3.8 copy.83
  364.1 3.5 multiply_reduce_fusion.2
  369.0 1.6 convert_reduce_fusion.4
  371.5 2.9 fusion.49
  374.4 1.4 fusion.41
  375.9 8.1 fusion.42
  384.1 7.0 multiply_reduce_fusion.1
  391.2 10.0 %multiply_convert_fusion.1 = bf16[12,512,512]{1,2,0:T(8,128)(2,1)S(1)} fusion(f32[12,512,512]{1,2,0:T(8,128)} %get-tuple-element.130, f32[12,512]{1,0:T(8,128)S(1)} %get-tuple-element.129, f32[12,512]{1,0:T(8,128)S(1)} %copy-done.28, f32[12,512,512]{1,2,0:T(8,128)} %copy-done.1, pred[512,512]{0,1:T(8,128)(4,1)S(1)} %iota_compare_fusion.1), kind=kLoop, calls=%fused_computation.21 | loop fusion | flops 22020096 | bytes 31768576 | tf_op jit(solution)/shard_map/while/body/eval_jaxpr/convert_element_type | solution.py:143
  401.3 3.2 multiply_bitcast_fusion
  404.6 22.1 %multiply_reduce_fusion = (f32[12,512]{1,0:T(8,128)S(1)}, f32[12,512,1024]{2,1,0:T(8,128)}) fusion(f32[12,512]{1,0:T(8,128)S(1)} %log_add_fusion, f32[12,512,1024]{2,1,0:T(8,128)} %get-tuple-element.124, pred[512,1024]{1,0:T(8,128)(4,1)S(1)} %copy-done.16, bf16[512,12,64]{0,2,1:T(8,128)(2,1)S(1)} %bitcast.90, bf16[1024,12,64]{0,2,1:T(8,128)(2,1)S(1)} %bitcast.84), kind=kOutput, calls=%fused_computation.1 | convolution fusion | flops 843048960 | bytes 53264384 | tf_op jit(solution)/shard_map/while/body/eval_jaxpr/qhd,khd->hqk/dot_general | solution.py:139
  426.8 18.1 %multiply_convert_fusion = bf16[12,512,1024]{2,1,0:T(8,128)(2,1)S(1)} fusion(f32[12,512,1024]{2,1,0:T(8,128)} %get-tuple-element.132, f32[12,512]{1,0:T(8,128)S(1)} %get-tuple-element.131, f32[12,512]{1,0:T(8,128)S(1)} %log_add_fusion, f32[12,512,1024]{2,1,0:T(8,128)} %get-tuple-element.124, pred[512,1024]{1,0:T(8,128)(4,1)} %iota_compare_fusion), kind=kLoop, calls=%fused_computation | loop fusion | flops 44040192 | bytes 63488000 | tf_op jit(solution)/shard_map/while/body/eval_jaxpr/convert_element_type | solution.py:143
  444.9 6.2 fusion.45
  451.1 4.0 fusion.38
  455.2 4.6 fusion.46
  460.1 12.8 %fusion.37 = bf16[1024,12,64]{0,2,1:T(8,128)(2,1)S(1)} fusion(f32[512,12,64]{0,2,1:T(8,128)S(1)} %copy-done.56, bf16[512,12,64]{0,2,1:T(8,128)(2,1)S(1)} %bitcast.91, f32[12,512]{1,0:T(8,128)S(1)} %log_add_fusion, f32[12,512,1024]{2,1,0:T(8,128)} %get-tuple-element.124, pred[512,1024]{1,0:T(8,128)(4,1)S(1)} %copy-done.17), kind=kOutput, calls=%fused_computation.65 | convolution fusion | flops 838336512 | bytes 29646848 | tf_op jit(solution)/shard_map/while/body/eval_jaxpr/hqk,qhd->khd/dot_general | solution.py:136
  474.1 7.0 fusion.71
  481.2 1.3 copy-done.12
  482.5 14.0 %fusion.47 = f32[3072,768]{1,0:T(8,128)} fusion(bf16[1024,768]{0,1:T(8,128)(2,1)S(1)} %copy-done.12, f32[1024]{0:T(1024)S(1)} %fusion.52, f32[1024,3072]{1,0:T(8,128)} %fusion.22, f32[3072]{0:T(1024)S(1)} %copy-done.44), kind=kOutput, calls=%fused_computation.93 | convolution fusion | flops 4866441216 | bytes 23609344 | tf_op jit(solution)/shard_map/dot_general | solution.py:44
  497.2 10.7 %fusion.75 = f32[768,3072]{1,0:T(8,128)} fusion(bf16[1024,3072]{1,0:T(8,128)(2,1)} %get-tuple-element.138, f32[1024,768]{0,1:T(8,128)} %copy-done.7, f32[768]{0:T(1024)S(1)} %copy-done.47, f32[768]{0:T(1024)S(1)} %convert_element_type.144, f32[1024]{0:T(1024)S(1)} %copy-done.40, f32[1024]{0:T(1024)S(1)} %broadcast_multiply_fusion), kind=kOutput, calls=%fused_computation.135 | convolution fusion | flops 4835770368 | bytes 18888704 | tf_op jit(solution)/shard_map/dot_general | solution.py:44
  508.6 12.4 %add_convert_fusion.2 = bf16[1024,768]{0,1:T(8,128)(2,1)} fusion(f32[1024,768]{0,1:T(8,128)} %copy-done.7, bf16[3072,768]{1,0:T(8,128)(2,1)} %all-gather.9.cloned.1.call-done, f32[768]{0:T(1024)S(1)} %convert_element_type.149, f32[1024,3072]{1,0:T(8,128)} %fusion.22, f32[3072]{0:T(1024)S(1)} %copy-done.44), kind=kOutput, calls=%fused_computation.77 | convolution fusion | flops 4866441216 | bytes 22035456 | tf_op jit(solution)/shard_map/dot_general | solution.py:40
  520.9 2.6 copy.90
  523.5 9.2 %fusion.84 = (f32[768]{0:T(1024)S(1)}, f32[1024,768]{1,0:T(8,128)}) fusion(bf16[768,2304]{1,0:T(8,128)(2,1)} %all-gather.5.cloned.1.call-done, bf16[1024,768]{0,1:T(8,128)(2,1)} %bitcast.86, bf16[1024,768]{0,1:T(8,128)(2,1)} %bitcast.76, bf16[1024,768]{0,1:T(8,128)(2,1)} %bitcast.81), kind=kOutput, calls=%fused_computation.142 | convolution fusion | flops 3638820096 | bytes 11406336 | tf_op jit(solution)/shard_map/dot_general | solution.py:50
  532.8 3.6 copy.87
  536.4 3.1 convert_reduce_fusion.1
  540.4 1.3 fusion.33
  541.8 41.5 %all-reduce.18 = (f32[768]{0:T(1024)S(1)}, f32[768]{0:T(1024)S(1)}, f32[1536]{0:T(1024)S(1)}, f32[768]{0:T(1024)S(1)}, f32[768]{0:T(1024)S(1)}, /*index=5*/f32[7...) all-reduce(f32[768]{0:T(1024)S(1)} %get-tuple-element.88, ...), channel_id=2, replica_groups=mesh['wide'=8,'narrow'=4] {'wide','narrow'}, use_global_device_ids=true, to_apply=%region_15.16.clone | all-reduce | flops 9216 | bytes 73728
  586.8 5.6 add_convert_fusion.1
  592.4 2.6 copy.91
  596.1 19.3 %reduce-scatter.5.cloned.1.call-done = f32[24,2304]{1,0:T(8,128)} async-done(((f32[768,2304]{1,0:T(8,128)}), f32[24,2304]{1,0:T(8,128)}) %reduce-scatter.5.cloned.1.call-update) | async-done | bytes 221200 | tf_op jit(solution)/shard_map/reduce_scatter | solution.py:301
  615.4 141.2 %reduce-scatter.11.cloned.1.call-done = f32[96,768]{1,0:T(8,128)} async-done(((f32[3072,768]{1,0:T(8,128)}), f32[96,768]{1,0:T(8,128)}) %reduce-scatter.11.cloned.1.call-update) | async-done | bytes 294928 | tf_op jit(solution)/shard_map/reduce_scatter | solution.py:267
  756.7 142.1 %reduce-scatter.9.cloned.1.call-done = f32[24,3072]{1,0:T(8,128)} async-done(((f32[768,3072]{1,0:T(8,128)}), f32[24,3072]{1,0:T(8,128)}) %reduce-scatter.9.cloned.1.call-update) | async-done | bytes 294928 | tf_op jit(solution)/shard_map/reduce_scatter | solution.py:265
  (202 shorter events, 30.9 us)
Async XLA Ops:
  7.2 67.7 %copy-start.21 = (bf16[1024,768]{1,0:T(8,128)(2,1)S(1)}, bf16[1024,768]{1,0:T(8,128)(2,1)}, u32[]{:S(2)}) copy-start(bf16[1024,768]{1,0:T(8,128)(2,1)} %param.15) | copy-start | bytes 4718596
  7.2 106.2 %all-gather.5.cloned.1.call-start = ((), (), s32[]{:S(2)}) async-start(), calls=%async_computation.4 | async-start | bytes 3649536 | tf_op jit(solution)/shard_map/all_gather | solution.py:194
  7.9 212.5 %all-gather.7.cloned.1.call-start = ((), (), s32[]{:S(2)}) async-start(), calls=%async_computation.5 | async-start | bytes 1216512 | tf_op jit(solution)/shard_map/all_gather | solution.py:196
  8.7 276.0 %all-gather.9.cloned.1.call-start = ((), (), s32[]{:S(2)}) async-start(), calls=%async_computation.6 | async-start | bytes 4866048 | tf_op jit(solution)/shard_map/all_gather | solution.py:227
  9.4 340.5 %all-gather.11.cloned.1.call-start = ((), (), s32[]{:S(2)}) async-start(), calls=%async_computation.7 | async-start | bytes 4866048 | tf_op jit(solution)/shard_map/all_gather | solution.py:242
  9.5 1.7 collective-permute-start
  12.2 10.3 %collective-permute-start.1 = (bf16[48,3072]{1,0:T(8,128)(2,1)S(1)}, bf16[48,3072]{1,0:T(8,128)(2,1)S(1)}, u32[]{:S(2)}, u32[]{:S(2)}) collective-permute-start(bf16[48,3072]{1,0:T(8,128)(2,1)S(1)} %maximum_select_fusion.5), channel_id=1, source_target_pairs={{0,2},{1,3},{2,0},{3,1},{4,6},{5,7},{6,4},{7,5},{8,10},{9,11},{10,... | collective-permute-start | bytes 884744 | tf_op jit(solution)/shard_map/ppermute | solution.py:19
  15.2 580.9 %reduce-scatter.7.cloned.1.call-start = ((), (), s32[]{:S(2)}) async-start(), calls=%async_computation.9 | async-start | bytes 2433024 | tf_op jit(solution)/shard_map/reduce_scatter | solution.py:303
  23.4 54.6 %collective-permute-start.2 = (bf16[96,3072]{1,0:T(8,128)(2,1)}, bf16[96,3072]{1,0:T(8,128)(2,1)}, u32[]{:S(2)}, u32[]{:S(2)}) collective-permute-start(bf16[96,3072]{1,0:T(8,128)(2,1)} %maximum_select_fusion.4), channel_id=1, source_target_pairs={{0,4},{1,5},{2,6},{3,7},{4,0},{5,1},{6,2},{7,3},{8,12},{9,13},{10,... | collective-permute-start | bytes 1769480 | tf_op jit(solution)/shard_map/ppermute | solution.py:19
  73.6 39.8 %copy-start.31 = (f32[768]{0:T(1024)}, f32[768]{0:T(1024)S(1)}, u32[]{:S(2)}) copy-start(f32[768]{0:T(1024)S(1)} %convert_element_type.133) | copy-start | bytes 9220
  73.6 39.7 %copy-start.48 = (f32[768]{0:T(1024)}, f32[768]{0:T(1024)S(1)}, u32[]{:S(2)}) copy-start(f32[768]{0:T(1024)S(1)} %convert_element_type.134) | copy-start | bytes 9220
  75.6 144.8 %copy-start.3 = (bf16[1024,768]{0,1:T(8,128)(2,1)}, bf16[1024,768]{0,1:T(8,128)(2,1)S(1)}, u32[]{:S(2)}) copy-start(bf16[1024,768]{0,1:T(8,128)(2,1)S(1)} %copy.73) | copy-start | bytes 4718596
  77.9 206.8 %copy-start.10 = (bf16[1024,768]{0,1:T(8,128)(2,1)}, bf16[1024,768]{0,1:T(8,128)(2,1)S(1)}, u32[]{:S(2)}) copy-start(bf16[1024,768]{0,1:T(8,128)(2,1)S(1)} %copy.82) | copy-start | bytes 4718596
  80.5 29.5 %collective-permute-start.3 = (bf16[192,3072]{1,0:T(8,128)(2,1)S(1)}, bf16[192,3072]{1,0:T(8,128)(2,1)S(1)}, u32[]{:S(2)}, u32[]{:S(2)}) collective-permute-start(bf16[192,3072]{1,0:T(8,128)(2,1)S(1)} %maximum_select_fusion.3), channel_id=1, source_target_pairs={{0,8},{1,9},{2,10},{3,11},{4,12},{5,13},{6,14},{7,15},{8,0},{9,1},... | collective-permute-start | bytes 3538952 | tf_op jit(solution)/shard_map/ppermute | solution.py:19
  82.3 31.1 %copy-start.29 = (f32[1024]{0:T(1024)}, f32[1024]{0:T(1024)S(1)}, u32[]{:S(2)}) copy-start(f32[1024]{0:T(1024)S(1)} %broadcast_multiply_fusion.1) | copy-start | bytes 12292
  82.7 37.1 %copy-start.37 = (f32[1024]{0:T(1024)}, f32[1024]{0:T(1024)S(1)}, u32[]{:S(2)}) copy-start(f32[1024]{0:T(1024)S(1)} %fusion.34) | copy-start | bytes 12292
  82.7 37.1 %copy-start.33 = (f32[1024]{0:T(1024)}, f32[1024]{0:T(1024)S(1)}, u32[]{:S(2)}) copy-start(f32[1024]{0:T(1024)S(1)} %fusion.53) | copy-start | bytes 12292
  111.9 113.9 %collective-permute-start.4 = (bf16[384,3072]{1,0:T(8,128)(2,1)}, bf16[384,3072]{1,0:T(8,128)(2,1)}, u32[]{:S(2)}, u32[]{:S(2)}) collective-permute-start(bf16[384,3072]{1,0:T(8,128)(2,1)} %maximum_select_fusion.2), channel_id=1, source_target_pairs={{0,16},{1,17},{2,18},{3,19},{4,20},{5,21},{6,22},{7,23},{8,24},{9,... | collective-permute-start | bytes 7077896 | tf_op jit(solution)/shard_map/ppermute | solution.py:19
  141.4 4.6 copy-start.1
  146.1 14.4 %copy-start.15 = (pred[512,1024]{1,0:T(8,128)(4,1)S(1)}, pred[512,1024]{1,0:T(8,128)(4,1)}, u32[]{:S(2)}) copy-start(pred[512,1024]{1,0:T(8,128)(4,1)} %iota_compare_fusion) | copy-start | bytes 1572868
  160.5 15.5 %copy-start = (f32[12,512,1024]{2,1,0:T(8,128)S(1)}, f32[12,512,1024]{2,1,0:T(8,128)}, u32[]{:S(2)}) copy-start(f32[12,512,1024]{2,1,0:T(8,128)} %get-tuple-element.124) | copy-start | bytes 75497472
  176.0 9.9 %copy-start.24 = (bf16[512,768]{0,1:T(8,128)(2,1)S(1)}, bf16[512,768]{0,1:T(8,128)(2,1)}, u32[]{:S(2)}) copy-start(bf16[512,768]{0,1:T(8,128)(2,1)} %copy.74) | copy-start | bytes 2359300
  224.3 1.7 copy-start.7
  224.4 1.7 copy-start.46
  225.9 58.9 %copy-start.44 = (f32[3072]{0:T(1024)S(1)}, f32[3072]{0:T(1024)}, u32[]{:S(2)}) copy-start(f32[3072]{0:T(1024)} %convert_element_type.147) | copy-start | bytes 36868
  360.3 3.8 copy-start.8
  360.3 3.8 copy-start.40
  364.1 3.5 copy-start.9
  367.6 1.4 copy-start.11
  368.5 2.1 copy-start.6
  368.5 2.1 copy-start.35
  369.0 2.0 copy-start.54
  369.0 2.5 copy-start.55
  371.5 2.9 copy-start.52
  371.5 2.9 copy-start.53
  374.4 1.5 copy-start.28
  374.4 9.7 %slice-start = ((s8[12582912]{0:T(1024)(128)(4,1)}), s8[4194304]{0:T(1024)(128)(4,1)S(1)}, s32[]{:S(2)}) async-start(s8[12582912]{0:T(1024)(128)(4,1)} %bitcast.67), calls=%async_computation.12 | async-start | bytes 8388608
  375.8 8.3 slice-start.1
  375.9 28.7 %copy-start.26 = (bf16[512,768]{0,1:T(8,128)(2,1)}, bf16[512,768]{0,1:T(8,128)(2,1)S(1)}, u32[]{:S(2)}) copy-start(bf16[512,768]{0,1:T(8,128)(2,1)S(1)} %get-tuple-element.117) | copy-start | bytes 2359300
  375.9 8.1 slice-start.2
  375.9 8.1 copy-start.25
  391.1 224.3 %reduce-scatter.5.cloned.1.call-start = ((), (), s32[]{:S(2)}) async-start(), calls=%async_computation.8 | async-start | bytes 7299072 | tf_op jit(solution)/shard_map/reduce_scatter | solution.py:301
  391.2 10.1 %copy-start.18 = (bf16[512,768]{0,1:T(8,128)(2,1)S(1)}, bf16[512,768]{0,1:T(8,128)(2,1)}, u32[]{:S(2)}) copy-start(bf16[512,768]{0,1:T(8,128)(2,1)} %copy.75) | copy-start | bytes 2359300
  401.2 3.4 copy-start.2
  401.2 3.4 copy-start.16
  401.2 3.4 copy-start.22
  451.1 4.0 copy-start.13
  455.2 17.7 %copy-start.14 = (bf16[1024,12,64]{0,2,1:T(8,128)(2,1)}, bf16[1024,12,64]{0,2,1:T(8,128)(2,1)S(1)}, u32[]{:S(2)}) copy-start(bf16[1024,12,64]{0,2,1:T(8,128)(2,1)S(1)} %fusion.38) | copy-start | bytes 4718596
  455.2 4.6 copy-start.20
  455.2 4.8 copy-start.17
  455.2 4.8 copy-start.27
  455.2 4.8 copy-start.56
  460.0 12.9 %copy-start.19 = (bf16[1024,12,64]{0,2,1:T(8,128)(2,1)}, bf16[1024,12,64]{0,2,1:T(8,128)(2,1)S(1)}, u32[]{:S(2)}) copy-start(bf16[1024,12,64]{0,2,1:T(8,128)(2,1)S(1)} %pad_maximum_fusion.1) | copy-start | bytes 4718596
  460.0 14.0 %copy-start.4 = (bf16[1024,768]{0,1:T(8,128)(2,1)S(1)}, bf16[1024,768]{0,1:T(8,128)(2,1)}, u32[]{:S(2)}) copy-start(bf16[1024,768]{0,1:T(8,128)(2,1)} %copy-done.3) | copy-start | bytes 4718596
  460.1 14.0 %copy-start.30 = (f32[1024]{0:T(1024)S(1)}, f32[1024]{0:T(1024)}, u32[]{:S(2)}) copy-start(f32[1024]{0:T(1024)} %copy-done.29) | copy-start | bytes 12292
  460.1 14.0 %copy-start.32 = (f32[768]{0:T(1024)S(1)}, f32[768]{0:T(1024)}, u32[]{:S(2)}) copy-start(f32[768]{0:T(1024)} %copy-done.31) | copy-start | bytes 9220
  460.1 14.0 %copy-start.34 = (f32[1024]{0:T(1024)S(1)}, f32[1024]{0:T(1024)}, u32[]{:S(2)}) copy-start(f32[1024]{0:T(1024)} %copy-done.33) | copy-start | bytes 12292
  460.1 14.0 %copy-start.49 = (f32[768]{0:T(1024)S(1)}, f32[768]{0:T(1024)}, u32[]{:S(2)}) copy-start(f32[768]{0:T(1024)} %copy-done.48) | copy-start | bytes 9220
  481.1 1.4 copy-start.12
  481.1 275.5 %reduce-scatter.11.cloned.1.call-start = ((), (), s32[]{:S(2)}) async-start(), calls=%async_computation.11 | async-start | bytes 9732096 | tf_op jit(solution)/shard_map/reduce_scatter | solution.py:267
  496.6 402.2 %reduce-scatter.9.cloned.1.call-start = ((), (), s32[]{:S(2)}) async-start(), calls=%async_computation.10 | async-start | bytes 9732096 | tf_op jit(solution)/shard_map/reduce_scatter | solution.py:265
  536.4 3.4 copy-start.5
  540.3 1.4 copy-start.41
  540.4 46.4 %copy-start.36 = (f32[1024]{0:T(1024)S(1)}, f32[1024]{0:T(1024)}, u32[]{:S(2)}) copy-start(f32[1024]{0:T(1024)} %copy-done.35) | copy-start | bytes 12292
  (9 other events, 10.3 us)
Sparse Core Ops, SparseCore 0:
  10.9 63.1 all-gather.4
  77.0 143.3 all-gather.6
  223.3 61.3 all-gather.8
  287.5 62.3 all-gather.10
  391.2 97.8 reduce-scatter.6
  496.1 119.2 reduce-scatter.4
  621.9 134.7 reduce-scatter.10
  764.2 134.5 reduce-scatter.8
